TPU v7x, 512 devices: a whole 4x8x8 slice. The times are simulated.
512 devices in a mesh: req: 64 (over z, x, core), tp: 8 (over y).
Axes of the slice: x: 4, y: 8, z: 8, core: 2. Of those that a mesh axis runs over, the one named last changes fastest.
Arguments:
- queries: bfloat16 [1024, 2560], P('req', 'tp'), may hold values from -64 to 64
- fresh_kv: bfloat16 [1024, 1280], P('req', 'tp'), may hold values from -9 to 9
- kv_cache: bfloat16 [8, 160, 655360], P('tp', None, 'req'), may hold values from -6 to 6
- out_weight: bfloat16 [2560, 2560], P('tp'), may hold values from -1.1953125 to 1.1953125
- offsets: int32 [1024], replicated, may hold values from 0 to 655358, as said below
- lengths: int32 [1024], replicated, may hold values from 2 to 8192, as said below
Outputs:
- mixed_out: bfloat16 [1024, 2560], P('req', 'tp')
Inputs may be any that keep to these rules, and one draw needn't show every extreme that they name: Request r belongs to index floor(r / 16) of req and its cache to index floor(offsets[r] / 10240), where it lies whole: offsets[r] + lengths[r] <= (floor(offsets[r] / 10240) + 1) * 10240; caches never intersect. The first 8 requests of each index have their caches on that index; every index holds the caches of exactly 8 requests of other indices, and those of one index's other requests lie on distinct indices. `lengths`: on every index of req one held cache has exactly 8192 tokens.
All inputs are finite; a program needn't handle non-finite values.
Results may differ from a plain program's by a relative error of at most 0.019.
Values may be sent and summed in bfloat16 or wider, within the bound.
No kernel may reach another device: no remote copies, remote signals or barrier semaphores. Data moves between devices by JAX's collectives and lax.ppermute only.
A program may use at most 64 MiB of HBM per device.

v0:
```python
import jax
import jax.numpy as jnp
from jax import lax
from jax.sharding import PartitionSpec as P

HD = 80
W = 4096


def attend(queries, fresh_kv, cache_block, starts, lengths):
    row_count = queries.shape[0]
    kv_heads = cache_block.shape[0]
    tokens = cache_block.shape[2]
    score_scale = HD ** (-0.5)
    grouped = queries.reshape(row_count, kv_heads, -1, HD)
    fresh_split = fresh_kv.reshape(row_count, kv_heads, 2, HD)
    scores = (
        jnp.einsum(
            "nhgd,hdt->hngt", grouped, cache_block[:, :HD, :], preferred_element_type=jnp.float32
        )
        * score_scale
    )
    positions = jnp.arange(tokens, dtype=jnp.int32)[None, :]
    window_end = (starts + lengths)[:, None]
    inside = (
        (positions >= starts[:, None])
        & (positions < window_end)
        & (positions >= window_end - (W - 1))
    )
    scores = jnp.where(inside[None, :, None, :], scores, -jnp.inf)
    own_score = (
        jnp.einsum(
            "nhgd,nhd->hng", grouped, fresh_split[:, :, 0, :], preferred_element_type=jnp.float32
        )
        * score_scale
    )
    highest = jnp.maximum(jnp.max(scores, axis=3), own_score)
    weights = jnp.exp(scores - highest[..., None])
    own_weight = jnp.exp(own_score - highest)
    totals = jnp.sum(weights, axis=3) + own_weight
    summed = jnp.einsum(
        "hngt,hdt->nhgd",
        weights.astype(jnp.bfloat16),
        cache_block[:, HD:, :],
        preferred_element_type=jnp.float32,
    )
    summed = summed + jnp.einsum(
        "hng,nhd->nhgd",
        own_weight.astype(jnp.bfloat16),
        fresh_split[:, :, 1, :],
        preferred_element_type=jnp.float32,
    )
    normed = summed / jnp.transpose(totals, (1, 0, 2))[..., None]
    return normed.astype(jnp.bfloat16).reshape(row_count, -1)


def shards(queries, fresh_kv, kv_cache, out_weight, offsets, lengths):
    devices = lax.axis_size("req")
    device_index = lax.axis_index("req")
    row_count = queries.shape[0]
    half_rows = row_count // 2
    shard_tokens = kv_cache.shape[2]
    shard_start = device_index * shard_tokens
    owner_table = (offsets // shard_tokens).reshape(devices, row_count)
    far_owners = owner_table[:, half_rows:]
    my_owners = lax.dynamic_slice_in_dim(far_owners, device_index, 1, 0)[0]
    home_first = device_index * row_count
    local_out = attend(
        queries[:half_rows],
        fresh_kv[:half_rows],
        kv_cache,
        lax.dynamic_slice_in_dim(offsets, home_first, half_rows) - shard_start,
        lax.dynamic_slice_in_dim(lengths, home_first, half_rows),
    )
    sent_queries, sent_fresh = (
        lax.all_gather(queries[half_rows:], "req", axis=0, tiled=True),
        lax.all_gather(fresh_kv[half_rows:], "req", axis=0, tiled=True),
    )
    flat_owners = far_owners.reshape(-1)
    picked = jnp.nonzero(flat_owners == device_index, size=half_rows)[0].astype(jnp.int32)
    request_ids = picked // half_rows * row_count + half_rows + picked % half_rows
    held_out = attend(
        jnp.take(sent_queries, picked, axis=0),
        jnp.take(sent_fresh, picked, axis=0),
        kv_cache,
        jnp.take(offsets, request_ids) - shard_start,
        jnp.take(lengths, request_ids),
    )
    returned = lax.all_gather(held_out, "req", axis=0, tiled=True)
    ordinal = device_index * half_rows + jnp.arange(half_rows, dtype=jnp.int32)
    earlier = jnp.arange(devices * half_rows, dtype=jnp.int32)[None, :] < ordinal[:, None]
    match_owner = flat_owners[None, :] == my_owners[:, None]
    rank_list = jnp.sum((earlier & match_owner).astype(jnp.int32), axis=1)
    remote_out = jnp.take(returned, my_owners * half_rows + rank_list, axis=0)
    attended = jnp.concatenate([local_out, remote_out], axis=0)
    partial_value = jnp.dot(attended, out_weight, preferred_element_type=jnp.float32)
    return lax.psum_scatter(
        partial_value.astype(jnp.bfloat16), "tp", scatter_dimension=1, tiled=True
    )


def solution(mesh):
    in_specs = (P("req", "tp"), P("req", "tp"), P("tp", None, "req"), P("tp", None), P(), P())
    out_specs = P("req", "tp")
    return jax.shard_map(shards, mesh=mesh, in_specs=in_specs, out_specs=out_specs, check_vma=False)
```

profile of v0, /device:TPU:2, one launch (start us, length us, event | category | flops | bytes accessed | tf_op | source)
XLA Modules:
  0.0 219.1 jit_solution(9321281883849411793)
XLA Ops:
  6.5 0.0 copy-start
  6.5 0.0 copy-start.1
  6.5 0.0 reduce-scatter.4.cloned.1.call-start
  6.5 0.8 add_select_fusion
  7.4 0.1 reshape.393
  7.4 0.7 fusion.70
  8.2 0.1 reshape.401
  8.3 0.3 reduce-window.12
  8.6 0.1 slice.49
  8.7 0.1 slice_reduce_fusion
  8.8 0.1 broadcast_add_fusion
  8.9 4.1 %scatter_custom_fusion = s32[8]{0:T(128)S(1)} fusion(s32[512]{0:T(512)S(1)} %bitcast.126, s32[512]{0:T(512)S(1)} %broadcast.332, s32[]{:T(128)} %constant.114.clone.1), kind=kCustom, calls=%fused_computation.118 | custom fusion | flops 512 | bytes 36 | tf_op jit(solution)/shard_map/scatter-add | solution.py:80
  13.0 0.2 select_n.123
  13.1 0.7 fusion.64
  13.8 0.7 compare_and_fusion.1
  14.5 0.7 fusion.72
  15.2 0.1 reshape.388
  15.3 0.7 fusion.71
  16.0 0.1 reshape.386
  16.1 0.1 fusion.55
  16.2 0.1 copy.31
  16.3 0.1 eq.29
  16.4 0.2 convert_reduce_fusion
  16.7 1.3 gather_fusion.1
  18.0 0.0 copy-done.1
  18.0 0.6 gather_fusion.2
  18.6 50.0 %all_gather.10 = bf16[512,160]{1,0:T(8,128)(2,1)S(1)} all-gather(bf16[8,160]{1,0:T(8,128)(2,1)S(1)} %get-tuple-element.23), channel_id=1, replica_groups=mesh['req'=64,'tp'=8] {'req'}, dimensions={0}, use_global_device_ids=true | all-gather | bytes 166400 | tf_op jit(solution)/shard_map/all_gather | solution.py:77
  68.6 0.6 gather_fusion
  69.2 0.1 gather.13
  69.3 0.1 copy_select_fusion
  69.4 45.3 %all_gather.9 = bf16[512,320]{1,0:T(8,128)(2,1)S(1)} all-gather(bf16[8,320]{1,0:T(8,128)(2,1)S(1)} %get-tuple-element.21), channel_id=1, replica_groups=mesh['req'=64,'tp'=8] {'req'}, dimensions={0}, use_global_device_ids=true | all-gather | bytes 332800 | tf_op jit(solution)/shard_map/all_gather | solution.py:76
  114.6 0.6 gather_fusion.3
  115.2 0.1 broadcast_select_fusion.1
  115.3 0.1 reshape.396
  115.4 0.1 fusion.56
  115.5 0.1 copy.33
  115.6 0.8 broadcast_add_fusion.1
  116.3 0.2 fusion.47
  116.5 0.0 copy-start.2
  116.5 2.0 fusion.73
  118.6 0.4 fusion.14
  118.9 0.0 copy-done.2
  119.0 0.6 fusion.37
  119.6 0.1 reshape.399
  119.7 48.0 %all_gather.11 = bf16[512,320]{1,0:T(8,128)(2,1)S(1)} all-gather(bf16[8,320]{1,0:T(8,128)(2,1)S(1)} %reshape.399), channel_id=1, replica_groups=mesh['req'=64,'tp'=8] {'req'}, dimensions={0}, use_global_device_ids=true | all-gather | bytes 332800 | tf_op jit(solution)/shard_map/all_gather | solution.py:89
  167.7 0.2 fusion.45
  167.9 0.0 copy-start.3
  167.9 2.0 fusion.74
  169.9 0.4 fusion.12
  170.3 0.0 copy-done.3
  170.3 0.6 fusion.34
  171.0 0.1 reshape.392
  171.1 0.6 gather_fusion.4
  171.7 0.1 broadcast_select_fusion
  171.7 0.0 copy-done
  171.7 0.3 convolution_convert_fusion
  172.1 1.1 copy.34
  173.2 0.0 reduce-scatter.4.cloned.1.call-update
  173.2 37.5 %reduce-scatter.4.cloned.1.call-done = bf16[320,16]{1,0:T(8,128)(2,1)} async-done(((bf16[2560,16]{1,0:T(8,128)(2,1)}), bf16[320,16]{1,0:T(8,128)(2,1)}) %reduce-scatter.4.cloned.1.call-update) | async-done | bytes 10256
  210.7 1.6 copy.35
  (19 shorter events, 0.2 us)
Async XLA Ops:
  6.5 165.2 %copy-start = (bf16[320,2560]{1,0:T(8,128)(2,1)S(1)}, bf16[320,2560]{1,0:T(8,128)(2,1)}, u32[]{:S(2)}) copy-start(bf16[320,2560]{1,0:T(8,128)(2,1)} %param.13) | copy-start | bytes 4915204
  6.5 11.5 %copy-start.1 = (s32[1024]{0:T(1024)S(1)}, s32[1024]{0:T(1024)}, u32[]{:S(2)}) copy-start(s32[1024]{0:T(1024)} %param.15) | copy-start | bytes 12292
  6.5 204.1 %reduce-scatter.4.cloned.1.call-start = ((), (), s32[]{:S(2)}) async-start(), calls=%async_computation.1 | async-start | bytes 737280
  116.5 2.5 %copy-start.2 = (bf16[1,160,10240]{2,1,0:T(8,128)(2,1)S(1)}, bf16[1,160,10240]{2,1,0:T(8,128)(2,1)}, u32[]{:S(2)}) copy-start(bf16[1,160,10240]{2,1,0:T(8,128)(2,1)} %param.12) | copy-start | bytes 9830404
  167.9 2.5 %copy-start.3 = (bf16[1,160,10240]{2,1,0:T(8,128)(2,1)S(1)}, bf16[1,160,10240]{2,1,0:T(8,128)(2,1)}, u32[]{:S(2)}) copy-start(bf16[1,160,10240]{2,1,0:T(8,128)(2,1)} %param.12) | copy-start | bytes 9830404
Sparse Core Ops, SparseCore 0:
  173.3 37.2 reduce-scatter.3
where the time goes:
time: 219 us
  blocking collectives  143 us (65%)
  waiting for transfers between devices  37.5 us (17%)
  between operations  13.5 us (6%)
  other arithmetic  9.94 us (5%)
  local copies, waits for them, and re-layouts  8.9 us (4%)
  matrix products  5.93 us (3%)
    all_gather x1, blocking collectives, shards(): lax.all_gather(fresh_kv[half_rows:], 'req', axis=0, tiled=True)  50 us
    all_gather x1, blocking collectives, shards(): returned = lax.all_gather(held_out, 'req', axis=0, tiled=True)  48 us
    all_gather x1, blocking collectives, shards(): lax.all_gather(queries[half_rows:], 'req', axis=0, tiled=True)  45.3 us
    unnamed x2, waiting for transfers between devices  37.5 us
  transfers between devices with their start and end apart: 1, of which 1 were waited for; matrix products, arithmetic and copies ran while one was open for 0% of the time, Pallas kernels for 0%

commit v1 on v0

--- a/solution.py
+++ b/solution.py
@@ -72,8 +72,18 @@
         lax.dynamic_slice_in_dim(offsets, home_first, half_rows) - shard_start,
         lax.dynamic_slice_in_dim(lengths, home_first, half_rows),
     )
+
+    def attach_leaf(panel, link_axis):
+        inter = jnp.concatenate(
+            lax.all_to_all(
+                jnp.stack([panel for _ in range(lax.axis_size(link_axis))], axis=0), link_axis, 0, 0
+            ),
+            0,
+        )
+        return inter
+
     sent_queries, sent_fresh = (
-        lax.all_gather(queries[half_rows:], "req", axis=0, tiled=True),
+        attach_leaf(queries[half_rows:], "req"),
         lax.all_gather(fresh_kv[half_rows:], "req", axis=0, tiled=True),
     )
     flat_owners = far_owners.reshape(-1)

time: 219 us -> 180 us (0.82)
  blocking collectives: 143 us -> 91.7 us
  starting transfers between devices: 0.01 us -> 13.9 us
    all_gather x1 -> x0, blocking collectives: 45.3 us -> none  [shards(): lax.all_gather(queries[half_rows:], 'req', axis=0, tiled=True)]
    all_to_all x0 -> x1, starting transfers between devices: none -> 13.9 us  [attach_leaf(): lax.all_to_all(jnp.stack([panel for _ in range(lax.axis_size(link_axis))]...]
    all_gather x1, blocking collectives: 50 us -> 43.9 us  [shards(): lax.all_gather(fresh_kv[half_rows:], 'req', axis=0, tiled=True)]
  transfers between devices with their start and end apart: 1 -> 2, of which waited for: 1 -> 1; matrix products, arithmetic and copies ran while one was open for 0% -> 8% of each run, Pallas kernels for 0% -> 0%
where the time goes in v1:
time: 180 us
  blocking collectives  91.7 us (51%)
  waiting for transfers between devices  37.5 us (21%)
  starting transfers between devices  13.9 us (8%)
  between operations  13.6 us (8%)
  other arithmetic  9.13 us (5%)
  local copies, waits for them, and re-layouts  8.42 us (5%)
  matrix products  5.93 us (3%)
    all_gather x1, blocking collectives, shards(): returned = lax.all_gather(held_out, 'req', axis=0, tiled=True)  47.8 us
    all_gather x1, blocking collectives, shards(): lax.all_gather(fresh_kv[half_rows:], 'req', axis=0, tiled=True)  43.9 us
    unnamed x2, waiting for transfers between devices  37.5 us
    all_to_all x1, starting transfers between devices, attach_leaf(): lax.all_to_all(jnp.stack([panel for _ in range(lax.axis_size(link_axis))]...  13.9 us
    scatter-add x1, other arithmetic, shards(): jnp.nonzero(flat_owners == device_index, size=half_rows)[0]  4.09 us
    dot_general x2, matrix products, attend(): jnp.einsum('nhgd,hdt->hngt', grouped, cache_block[:, :HD, :], preferred_e...  4.07 us
  transfers between devices with their start and end apart: 2, of which 1 were waited for; matrix products, arithmetic and copies ran while one was open for 8% of the time, Pallas kernels for 0%

profile of v1, /device:TPU:2, one launch (start us, length us, event | category | flops | bytes accessed | tf_op | source)
XLA Modules:
  0.0 180.1 jit_solution(3478192577665686892)
XLA Ops:
  6.5 0.0 copy-start
  6.5 0.0 copy-start.1
  6.5 0.0 copy-start.5
  6.5 0.0 copy-start.2
  6.5 0.9 fusion.71
  7.4 0.8 stack.2
  8.2 13.9 %all-to-all-start = ((bf16[64,8,320]{2,1,0:T(8,128)(2,1)}), bf16[64,8,320]{2,1,0:T(8,128)(2,1)S(1)}, u32[]{:S(2)}, u32[]{:S(2)}) async-start(bf16[64,8,320]{2,1,0:T(8,128)(2,1)} %stack.2), calls=%async_computation | async-start | bytes 786432 | tf_op jit(solution)/shard_map/all_to_all | solution.py:78
  22.0 0.0 reduce-scatter.4.cloned.1.call-start
  22.1 0.7 add_select_fusion
  22.8 0.1 reshape.398
  22.9 0.7 fusion.70
  23.6 0.1 reshape.407
  23.7 0.3 reduce-window.12
  24.0 0.1 slice.49
  24.1 0.1 slice_reduce_fusion
  24.2 0.1 broadcast_add_fusion
  24.3 4.1 %scatter_custom_fusion = s32[8]{0:T(128)S(1)} fusion(s32[512]{0:T(512)S(1)} %bitcast.128, s32[512]{0:T(512)S(1)} %broadcast.334, s32[]{:T(128)} %constant.114.clone.1), kind=kCustom, calls=%fused_computation.118 | custom fusion | flops 512 | bytes 36 | tf_op jit(solution)/shard_map/scatter-add | solution.py:90
  28.4 0.2 select_n.123
  28.6 0.7 fusion.64
  29.2 0.7 compare_and_fusion.1
  29.9 0.0 copy-done.5
  29.9 0.1 reshape.393
  30.0 0.1 reshape.391
  30.1 0.1 fusion.55
  30.2 0.1 copy.31
  30.3 0.1 eq.29
  30.4 0.2 convert_reduce_fusion
  30.7 0.0 copy-done.1
  30.7 0.6 gather_fusion.1
  31.3 0.0 copy-done.2
  31.3 0.6 gather_fusion.2
  32.0 43.9 %all_gather.6 = bf16[512,160]{1,0:T(8,128)(2,1)S(1)} all-gather(bf16[8,160]{1,0:T(8,128)(2,1)S(1)} %get-tuple-element.23), channel_id=1, replica_groups=mesh['req'=64,'tp'=8] {'req'}, dimensions={0}, use_global_device_ids=true | all-gather | bytes 166400 | tf_op jit(solution)/shard_map/all_gather | solution.py:87
  75.8 0.6 gather_fusion
  76.4 0.1 gather.13
  76.5 0.1 broadcast_add_fusion.1
  76.5 0.2 fusion.45
  76.7 0.0 copy-start.3
  76.7 2.0 %fusion.74 = (f32[8,4]{0,1:T(4,128)S(1)}, f32[8,4,10240]{2,0,1:T(8,128)S(1)}) fusion(bf16[1,160,10240]{2,1,0:T(8,128)(2,1)} %param.12, bf16[8,4,80]{2,1,0:T(4,128)(2,1)S(1)} %reshape.391, pred[8,10240]{1,0:T(8,128)(4,1)S(1)} %fusion.45), kind=kOutput, calls=%fused_computation.127 | convolution fusion | flops 53411808 | bytes 3036288 | tf_op jit(solution)/shard_map/nhgd,hdt->hngt/dot_general | solution.py:18
  78.8 0.4 fusion.12
  79.2 0.0 copy-done.3
  79.2 0.6 fusion.34
  79.8 0.1 reshape.397
  79.9 0.2 fusion.47
  80.1 0.1 copy_select_fusion
  80.2 0.0 all-to-all-done
  80.2 0.6 gather_fusion.3
  80.8 0.1 broadcast_select_fusion.1
  80.9 0.1 reshape.402
  80.9 0.1 fusion.56
  81.1 0.1 copy.33
  81.1 2.0 %fusion.73 = (f32[8,4]{0,1:T(4,128)S(1)}, f32[8,4,10240]{2,0,1:T(8,128)S(1)}) fusion(bf16[1,160,10240]{2,1,0:T(8,128)(2,1)} %param.12, bf16[8,4,80]{2,1,0:T(4,128)(2,1)S(1)} %reshape.402, pred[8,10240]{1,0:T(8,128)(4,1)S(1)} %fusion.47), kind=kOutput, calls=%fused_computation.126 | convolution fusion | flops 53411808 | bytes 3036288 | tf_op jit(solution)/shard_map/nhgd,hdt->hngt/dot_general | solution.py:18
  83.2 0.4 fusion.14
  83.6 0.0 copy-done.4
  83.6 0.6 fusion.37
  84.2 0.1 reshape.405
  84.3 47.8 %all_gather.7 = bf16[512,320]{1,0:T(8,128)(2,1)S(1)} all-gather(bf16[8,320]{1,0:T(8,128)(2,1)S(1)} %reshape.405), channel_id=1, replica_groups=mesh['req'=64,'tp'=8] {'req'}, dimensions={0}, use_global_device_ids=true | all-gather | bytes 332800 | tf_op jit(solution)/shard_map/all_gather | solution.py:99
  132.2 0.6 gather_fusion.4
  132.7 0.1 broadcast_select_fusion
  132.8 0.0 copy-done
  132.8 0.3 convolution_convert_fusion
  133.2 1.1 copy.34
  134.3 0.0 reduce-scatter.4.cloned.1.call-update
  134.3 37.5 %reduce-scatter.4.cloned.1.call-done = bf16[320,16]{1,0:T(8,128)(2,1)} async-done(((bf16[2560,16]{1,0:T(8,128)(2,1)}), bf16[320,16]{1,0:T(8,128)(2,1)}) %reduce-scatter.4.cloned.1.call-update) | async-done | bytes 10256
  171.7 1.6 copy.35
  (21 shorter events, 0.2 us)
Async XLA Ops:
  6.5 126.3 %copy-start = (bf16[320,2560]{1,0:T(8,128)(2,1)S(1)}, bf16[320,2560]{1,0:T(8,128)(2,1)}, u32[]{:S(2)}) copy-start(bf16[320,2560]{1,0:T(8,128)(2,1)} %param.13) | copy-start | bytes 4915204
  6.5 24.1 %copy-start.1 = (s32[1024]{0:T(1024)S(1)}, s32[1024]{0:T(1024)}, u32[]{:S(2)}) copy-start(s32[1024]{0:T(1024)} %param.14) | copy-start | bytes 12292
  6.5 23.4 %copy-start.5 = (bf16[16,160]{1,0:T(8,128)(2,1)S(1)}, bf16[16,160]{1,0:T(8,128)(2,1)}, u32[]{:S(2)}) copy-start(bf16[16,160]{1,0:T(8,128)(2,1)} %param.11) | copy-start | bytes 15364
  6.5 24.8 %copy-start.2 = (s32[1024]{0:T(1024)S(1)}, s32[1024]{0:T(1024)}, u32[]{:S(2)}) copy-start(s32[1024]{0:T(1024)} %param.15) | copy-start | bytes 12292
  8.2 72.0 %all-to-all-start = ((bf16[64,8,320]{2,1,0:T(8,128)(2,1)}), bf16[64,8,320]{2,1,0:T(8,128)(2,1)S(1)}, u32[]{:S(2)}, u32[]{:S(2)}) async-start(bf16[64,8,320]{2,1,0:T(8,128)(2,1)} %stack.2), calls=%async_computation | async-start | bytes 786432 | tf_op jit(solution)/shard_map/all_to_all | solution.py:78
  22.0 149.7 %reduce-scatter.4.cloned.1.call-start = ((), (), s32[]{:S(2)}) async-start(), calls=%async_computation.2 | async-start | bytes 737280
  76.7 2.5 %copy-start.3 = (bf16[1,160,10240]{2,1,0:T(8,128)(2,1)S(1)}, bf16[1,160,10240]{2,1,0:T(8,128)(2,1)}, u32[]{:S(2)}) copy-start(bf16[1,160,10240]{2,1,0:T(8,128)(2,1)} %param.12) | copy-start | bytes 9830404
  81.1 2.4 %copy-start.4 = (bf16[1,160,10240]{2,1,0:T(8,128)(2,1)S(1)}, bf16[1,160,10240]{2,1,0:T(8,128)(2,1)}, u32[]{:S(2)}) copy-start(bf16[1,160,10240]{2,1,0:T(8,128)(2,1)} %param.12) | copy-start | bytes 9830404
Sparse Core Ops, SparseCore 0:
  134.4 37.2 reduce-scatter.3
